TPU v7x, 512 devices: a whole 4x4x16 slice. The times are simulated.
512 devices in a mesh: energy: 32 (over z_hi, y, core), cell: 16 (over x, z_lo).
Axes of the slice: x: 4, y: 4, z: 16 (z_hi: 4, z_lo: 4; z = z_hi * 4 + z_lo), core: 2. Of those that a mesh axis runs over, the one named last changes fastest.
Arguments:
- g_retarded: bfloat16 [2, 32, 16, 128, 2048], P(None, 'energy', None, None, 'cell'), may hold values from -0.75 to 0.75
- sigma_lesser: bfloat16 [2, 32, 128, 2048], P(None, 'energy', None, 'cell'), may hold values from -1.5 to 1.5
- w_screened: bfloat16 [2, 32, 16, 128, 2048], P(None, 'energy', None, None, 'cell'), may hold values from -0.75 to 0.75
- coupling: int32 [16, 16], replicated, may hold values 0 or 1
Outputs:
- polarization: bfloat16 [16, 2, 32, 16384], P('cell', None, 'energy')
- w_lesser: bfloat16 [16, 2, 32, 128, 128], P('cell', None, 'energy')
Inputs may be any that keep to these rules, and one draw needn't show every extreme that they name: coupling[i, j] is 1 where cell i is coupled to cell j and 0 elsewhere.
All inputs are finite; a program needn't handle non-finite values.
Results may differ from a plain program's by a relative error of at most 0.024.
Values may be sent and summed in bfloat16 or wider, within the bound.
A program may use at most 64 MiB of HBM per device.

v0:
```python
import math

import jax
import jax.numpy as jnp
from jax import lax
from jax.sharding import Mesh
from jax.sharding import PartitionSpec as P

ENERGY = ("energy_0", "energy_1", "energy_2")


def cut_along(x, dim, devices):
    lengths = x.shape
    parts = x.reshape(*lengths[:dim], devices, lengths[dim] // devices, *lengths[dim + 1 :])
    return jnp.moveaxis(parts, dim, 0)


def sent_and_summed(x, axis, dim):
    parts = cut_along(x, dim, lax.axis_size(axis))
    arrived = lax.all_to_all(parts, axis, split_axis=0, concat_axis=0, tiled=True)
    return arrived.astype(jnp.float32).sum(axis=0)


def laid_out(parts, dim):
    parts = jnp.moveaxis(parts, 0, dim)
    lengths = parts.shape
    return parts.reshape(*lengths[:dim], lengths[dim] * lengths[dim + 1], *lengths[dim + 2 :])


def moved_by_axis(parts, axes, sequence):
    inside = parts.shape[1:]
    out = parts.reshape(*(lax.axis_size(a) for a in axes), *inside)
    for k in sequence:
        out = lax.all_to_all(out, axes[k], k, k, tiled=True)
    return out.reshape(-1, *inside)


def exchange_by_chip(x, groups, sequence, split_dim, concat_dim):
    devices = lax.axis_size(groups[0]) * lax.axis_size(groups[1])
    parts = cut_along(x, split_dim, devices)
    return laid_out(moved_by_axis(parts, groups, sequence), concat_dim)


def forward_product(left, right):
    return jnp.einsum("eibjc,ecjd->eibjd", left, right, preferred_element_type=jnp.float32)


def adjoint_product(left, right):
    return jnp.einsum("eibjc,eidjc->iebd", left, right, preferred_element_type=jnp.float32)


def sandwich_rows(columns, sources, coupling, cell_index, count):
    orbitals = sources.shape[2]
    local_cells = sources.shape[3] // orbitals
    energies = sources.shape[1]
    rows_block = columns
    rows_block = rows_block.reshape(2, energies, count, orbitals, local_cells, orbitals)
    col_re = rows_block[0]
    col_im = rows_block[1]
    source = sources.reshape(2, energies, orbitals, local_cells, orbitals)
    src_re = source[0]
    src_im = source[1]
    mid_re = (forward_product(col_re, src_re) - forward_product(col_im, src_im)).astype(
        jnp.bfloat16
    )
    mid_im = (forward_product(col_re, src_im) + forward_product(col_im, src_re)).astype(
        jnp.bfloat16
    )
    weight = lax.dynamic_slice(coupling, (0, cell_index * local_cells), (count, local_cells))
    weight = weight.astype(jnp.bfloat16)[None, :, None, :, None]
    mid_re = mid_re * weight
    mid_im = mid_im * weight
    part_re = adjoint_product(mid_re, col_re) + adjoint_product(mid_im, col_im)
    part_im = adjoint_product(mid_im, col_re) - adjoint_product(mid_re, col_im)
    return jnp.stack([part_re, part_im], axis=1)


def correlate_spectral(spread):
    energies = spread.shape[2]
    length = 2 * energies
    freqs = jnp.arange(length, dtype=jnp.int32)[:, None]
    points = jnp.arange(energies, dtype=jnp.int32)[None, :]
    phase = jnp.mod(freqs * points, length).astype(jnp.float32) * (math.pi / energies)
    cos_table = jnp.cos(phase)
    sin_table = jnp.sin(phase)
    cos_high = cos_table.astype(jnp.bfloat16)
    cos_low = (cos_table - cos_high.astype(jnp.float32)).astype(jnp.bfloat16)
    sin_high = sin_table.astype(jnp.bfloat16)
    sin_low = (sin_table - sin_high.astype(jnp.float32)).astype(jnp.bfloat16)

    def forward(high, low, data):
        upper = jnp.einsum("ft,ctk->cfk", high, data, preferred_element_type=jnp.float32)
        return upper + jnp.einsum("ft,ctk->cfk", low, data, preferred_element_type=jnp.float32)

    def inverse(table, data):
        return jnp.einsum("ft,cfk->ctk", table, data, precision=lax.Precision.HIGH)

    low_re = spread[:, 0]
    low_im = spread[:, 1]
    high_re = spread[:, 2]
    high_im = spread[:, 3]
    spec_a_re = forward(cos_high, cos_low, low_re) + forward(sin_high, sin_low, low_im)
    spec_a_im = forward(cos_high, cos_low, low_im) - forward(sin_high, sin_low, low_re)
    spec_b_re = forward(cos_high, cos_low, high_re) + forward(sin_high, sin_low, high_im)
    spec_b_im = forward(cos_high, cos_low, high_im) - forward(sin_high, sin_low, high_re)
    cross_re = spec_a_re * spec_b_re + spec_a_im * spec_b_im
    cross_im = spec_a_im * spec_b_re - spec_a_re * spec_b_im
    back_re = (inverse(cos_table, cross_re) - inverse(sin_table, cross_im)) / length
    back_im = (inverse(cos_table, cross_im) + inverse(sin_table, cross_re)) / length
    factor = 1.0 / math.sqrt(energies)
    return jnp.stack([back_im * factor, -back_re * factor], axis=1)


def on_device(g_retarded, sigma_lesser, w_screened, coupling):
    cell_index = lax.axis_index("cell")
    orbitals = sigma_lesser.shape[2]
    local_cells = sigma_lesser.shape[3] // orbitals
    energies_dev = sigma_lesser.shape[1]
    lesser = sent_and_summed(
        sandwich_rows(
            g_retarded, sigma_lesser, coupling, cell_index, local_cells * lax.axis_size("cell")
        ).astype(jnp.bfloat16),
        "cell",
        0,
    )
    row_block = lax.dynamic_slice_in_dim(g_retarded, cell_index * local_cells + 0, 1, 2)
    blocks = [row_block[:, :, 0, :, 0:orbitals]]
    diagonal = jnp.stack(blocks, axis=0).astype(jnp.float32)
    diag_re = diagonal[:, 0]
    diag_im = diagonal[:, 1]
    greater = lesser + jnp.stack(
        [diag_re - jnp.swapaxes(diag_re, -1, -2), diag_im + jnp.swapaxes(diag_im, -1, -2)], axis=1
    )
    both = jnp.concatenate([lesser, greater], axis=1).astype(jnp.bfloat16)
    flat = both.reshape(local_cells, 4, energies_dev, orbitals * orbitals)
    spread = exchange_by_chip(flat, (("energy_0", "energy_1"), "energy_2"), (1, 0), 3, 2)
    polar = correlate_spectral(spread).astype(jnp.bfloat16)
    polar_local = lax.all_to_all(polar, ENERGY, split_axis=2, concat_axis=3, tiled=True)
    sources = polar_local.reshape(local_cells, 2, energies_dev, orbitals, orbitals)
    sources = jnp.transpose(sources, (1, 2, 3, 0, 4)).reshape(
        2, energies_dev, orbitals, local_cells * orbitals
    )
    screened = sent_and_summed(
        sandwich_rows(
            w_screened, sources, coupling, cell_index, local_cells * lax.axis_size("cell")
        ).astype(jnp.bfloat16),
        "cell",
        0,
    )
    return (polar_local, screened.astype(jnp.bfloat16))


def solution(mesh):
    finer = Mesh(
        mesh.devices.reshape(4, 4, 2, mesh.shape["cell"]),
        ("energy_0", "energy_1", "energy_2", "cell"),
    )
    placed = (
        P(None, ENERGY, None, None, "cell"),
        P(None, ENERGY, None, "cell"),
        P(None, ENERGY, None, None, "cell"),
        P(),
    )
    return jax.shard_map(
        on_device,
        mesh=finer,
        in_specs=placed,
        out_specs=(P("cell", None, ENERGY, None), P("cell", None, ENERGY, None, None)),
        check_vma=False,
    )
```

profile of v0, /device:TPU:1, one launch (start us, length us, event | category | flops | bytes accessed | tf_op | source)
XLA Modules:
  0.0 142.6 jit_solution(4928172760421186370)
XLA Ops:
  0.6 0.0 copy-start
  0.6 0.0 copy-start.2
  0.7 1.5 %fusion.58 = f32[128,16,128]{2,0,1:T(8,128)S(1)} fusion(bf16[2,1,16,128,128]{4,3,2,1,0:T(8,128)(2,1)} %param.4, bf16[2,1,128,128]{3,2,1,0:T(8,128)(2,1)} %param.5), kind=kOutput, calls=%fused_computation.79 | convolution fusion | flops 67108864 | bytes 1605632 | tf_op jit(solution)/shard_map/eibjc,ecjd->eibjd/dot_general | solution.py:45
  2.1 0.0 copy-done
  2.1 0.0 copy-start.3
  2.2 0.3 fusion.54
  2.5 0.4 copy-done.3
  2.8 0.2 fusion.126
  3.0 0.3 fusion.17
  3.4 0.5 fusion.56
  3.9 0.3 fusion.19
  4.2 0.5 fusion.52
  4.7 0.5 fusion.11
  5.3 0.5 fusion.10
  5.8 0.1 pad_maximum_fusion
  5.9 1.1 copy.85
  6.9 9.0 %all-to-all-start = ((bf16[16,1,2,1,128,128]{5,4,3,2,1,0:T(8,128)(2,1)}), bf16[16,1,2,1,128,128]{5,4,3,2,1,0:T(8,128)(2,1)S(1)}, u32[]{:S(2)}, u32[]{:S(2)}) async-start(bf16[16,1,2,1,128,128]{5,4,3,2,1,0:T(8,128)(2,1)} %copy.85), calls=%async_computation | async-start | bytes 2097152 | tf_op jit(solution)/shard_map/all_to_all | solution.py:20
  16.0 0.1 copy.86
  16.1 0.1 copy.87
  16.3 26.7 %all-to-all-done = bf16[16,1,2,1,128,128]{5,4,3,2,1,0:T(8,128)(2,1)S(1)} async-done(((bf16[16,1,2,1,128,128]{5,4,3,2,1,0:T(8,128)(2,1)}), bf16[16,1,2,1,128,128]{5,4,3,2,1,0:T(8,128)(2,1)S(1)}, u32[]{:S(2)}, u32[]{:S(2)}) %all-to-all-start) | async-done | bytes 1048608 | tf_op jit(solution)/shard_map/all_to_all | solution.py:20
  43.0 0.1 convert_reduce_fusion
  43.2 0.1 concatenate.55
  43.3 0.1 copy.88
  43.5 5.2 %all_to_all.32 = bf16[16,2,1,4,1,512]{5,0,3,4,2,1:T(8,128)(2,1)S(1)} all-to-all(bf16[16,2,1,4,1,512]{5,0,3,4,2,1:T(8,128)(2,1)S(1)} %copy.89), channel_id=1, replica_groups=mesh['energy_0'=4,'energy_1'=4,'energy_2'=2,'cell'=16] {'energy_2'}, dimensions={1} | all-to-all | bytes 262144 | tf_op jit(solution)/shard_map/all_to_all | solution.py:34
  48.7 0.1 copy.90
  48.8 28.7 %all_to_all.33 = bf16[16,2,1,4,1,512]{5,1,3,4,2,0:T(2,128)(2,1)S(1)} all-to-all(bf16[16,2,1,4,1,512]{5,1,3,4,2,0:T(2,128)(2,1)S(1)} %copy.90), channel_id=1, replica_groups=mesh['energy_0'=4,'energy_1'=4,'energy_2'=2,'cell'=16] {'energy_0','ener..., dimensions={0} | all-to-all | bytes 262144 | tf_op jit(solution)/shard_map/all_to_all | solution.py:34
  77.5 0.1 copy.91
  77.6 0.3 fusion.105
  77.8 0.3 fusion.106
  78.1 0.3 fusion.108
  78.4 0.3 fusion.102
  78.6 0.3 fusion.104
  78.9 0.3 fusion.109
  79.1 0.3 fusion.107
  79.4 0.3 fusion.103
  79.7 0.3 convolution_add_fusion.7
  79.9 0.3 convolution_add_fusion.9
  80.2 0.3 convolution_add_fusion.11
  80.5 0.3 convolution_add_fusion.5
  80.7 0.3 fusion.26
  81.0 0.3 fusion.27
  81.3 0.3 fusion.24
  81.5 0.3 multiply_subtract_fusion
  81.8 0.3 fusion.78
  82.2 0.3 fusion.80
  82.5 0.4 fusion.34
  82.9 0.4 fusion.35
  83.3 0.1 copy.93
  83.3 22.1 %all_to_all.34 = bf16[1,2,32,512]{3,1,0,2:T(2,128)(2,1)S(1)} all-to-all(bf16[1,2,32,512]{3,1,0,2:T(2,128)(2,1)S(1)} %copy.93), channel_id=1, replica_groups=mesh['energy_0'=4,'energy_1'=4,'energy_2'=2,'cell'=16] {'energy_0','ener..., dimensions={2} | all-to-all | bytes 131072 | tf_op jit(solution)/shard_map/all_to_all | solution.py:138
  105.5 0.3 slice_reduce_fusion.1
  105.8 0.3 fusion.46
  106.2 0.3 fusion.42
  106.5 0.3 fusion.21
  106.8 0.5 fusion.44
  107.3 0.3 fusion.23
  107.7 0.5 fusion.40
  108.2 0.5 fusion.9
  108.7 0.5 fusion.8
  109.2 0.1 pad_maximum_fusion.1
  109.3 1.1 copy.102
  110.4 3.7 %all-to-all-start.4 = ((bf16[16,1,2,1,128,128]{5,4,3,2,1,0:T(8,128)(2,1)}), bf16[16,1,2,1,128,128]{5,4,3,2,1,0:T(8,128)(2,1)S(1)}, u32[]{:S(2)}, u32[]{:S(2)}) async-start(bf16[16,1,2,1,128,128]{5,4,3,2,1,0:T(8,128)(2,1)} %copy.102), calls=%async_computation.4 | async-start | bytes 2097152 | tf_op jit(solution)/shard_map/all_to_all | solution.py:20
  114.1 27.2 %all-to-all-done.4 = bf16[16,1,2,1,128,128]{5,4,3,2,1,0:T(8,128)(2,1)S(1)} async-done(((bf16[16,1,2,1,128,128]{5,4,3,2,1,0:T(8,128)(2,1)}), bf16[16,1,2,1,128,128]{5,4,3,2,1,0:T(8,128)(2,1)S(1)}, u32[]{:S(2)}, u32[]{:S(2)}) %all-to-all-start.4) | async-done | bytes 1048608 | tf_op jit(solution)/shard_map/all_to_all | solution.py:20
  141.2 0.8 reduce_sum.27
  142.0 0.6 copy.124
  (17 shorter events, 0.3 us)
Async XLA Ops:
  0.6 1.5 %copy-start = (bf16[2,1,16,128,128]{4,3,2,1,0:T(8,128)(2,1)S(1)}, bf16[2,1,16,128,128]{4,3,2,1,0:T(8,128)(2,1)}, u32[]{:S(2)}) copy-start(bf16[2,1,16,128,128]{4,3,2,1,0:T(8,128)(2,1)} %param.4) | copy-start | bytes 3145732
  0.6 1.5 %copy-start.2 = (bf16[2,1,128,128]{3,2,1,0:T(8,128)(2,1)S(1)}, bf16[2,1,128,128]{3,2,1,0:T(8,128)(2,1)}, u32[]{:S(2)}) copy-start(bf16[2,1,128,128]{3,2,1,0:T(8,128)(2,1)} %param.5) | copy-start | bytes 196612
  2.1 0.7 copy-start.3
  6.9 36.1 %all-to-all-start = ((bf16[16,1,2,1,128,128]{5,4,3,2,1,0:T(8,128)(2,1)}), bf16[16,1,2,1,128,128]{5,4,3,2,1,0:T(8,128)(2,1)S(1)}, u32[]{:S(2)}, u32[]{:S(2)}) async-start(bf16[16,1,2,1,128,128]{5,4,3,2,1,0:T(8,128)(2,1)} %copy.85), calls=%async_computation | async-start | bytes 2097152 | tf_op jit(solution)/shard_map/all_to_all | solution.py:20
  81.5 24.3 %copy-start.1 = (bf16[2,1,16,128,128]{4,3,2,1,0:T(8,128)(2,1)S(1)}, bf16[2,1,16,128,128]{4,3,2,1,0:T(8,128)(2,1)}, u32[]{:S(2)}) copy-start(bf16[2,1,16,128,128]{4,3,2,1,0:T(8,128)(2,1)} %param.6) | copy-start | bytes 3145732
  110.4 30.8 %all-to-all-start.4 = ((bf16[16,1,2,1,128,128]{5,4,3,2,1,0:T(8,128)(2,1)}), bf16[16,1,2,1,128,128]{5,4,3,2,1,0:T(8,128)(2,1)S(1)}, u32[]{:S(2)}, u32[]{:S(2)}) async-start(bf16[16,1,2,1,128,128]{5,4,3,2,1,0:T(8,128)(2,1)} %copy.102), calls=%async_computation.4 | async-start | bytes 2097152 | tf_op jit(solution)/shard_map/all_to_all | solution.py:20
where the time goes:
time: 143 us
  blocking collectives  56 us (39%)
  waiting for transfers between devices  53.9 us (38%)
  matrix products  13.5 us (9%)
  starting transfers between devices  12.7 us (9%)
  local copies, waits for them, and re-layouts  4.2 us (3%)
    all_to_all x2, waiting for transfers between devices, sent_and_summed(): lax.all_to_all(parts, axis, split_axis=0, concat_axis=0, tiled=True)  53.9 us
    all_to_all x2, blocking collectives, moved_by_axis(): out = lax.all_to_all(out, axes[k], k, k, tiled=True)  33.9 us
    all_to_all x1, blocking collectives, on_device(): lax.all_to_all(polar, ENERGY, split_axis=2, concat_axis=3, tiled=True)  22.1 us
    all_to_all x2, starting transfers between devices, sent_and_summed(): lax.all_to_all(parts, axis, split_axis=0, concat_axis=0, tiled=True)  12.7 us
    dot_general x8, matrix products, adjoint_product(): jnp.einsum('eibjc,eidjc->iebd', left, right, preferred_element_type=jnp.f...  4.15 us
    dot_general x8, matrix products, forward_product(): jnp.einsum('eibjc,ecjd->eibjd', left, right, preferred_element_type=jnp.f...  3.74 us
  transfers between devices with their start and end apart: 2, of which 2 were waited for; matrix products, arithmetic and copies ran while one was open for 0% of the time, Pallas kernels for 0%

commit v1 on v0

v1 whole, which is shorter than its diff:
```python
import math

import jax
import jax.numpy as jnp
from jax import lax
from jax.experimental import pallas as pl
from jax.experimental.pallas import tpu as pltpu
from jax.sharding import PartitionSpec as P

ORB = 128
NX = 4
NZ = 4
NE = 32
F32 = jnp.float32
BF16 = jnp.bfloat16
MESH = pl.DeviceIdType.MESH

RIGHT = {("D", 0): 0, ("D", 1): 1, ("N", 2): 2, ("N", 3): 3, ("C", 0): 4, ("C", 1): 5}
LEFT = {("D", 2): 6, ("D", 3): 7, ("N", 0): 8, ("N", 1): 9, ("C", 2): 10, ("C", 3): 11}
UNITS = {**RIGHT, **LEFT}


def dot(a, b):
    return lax.dot_general(a, b, (((1,), (0,)), ((), ())), preferred_element_type=F32)


def dot_t(a, b):
    return lax.dot_general(a, b, (((1,), (1,)), ((), ())), preferred_element_type=F32)


def stacked(re, im):
    top = jnp.concatenate([re, im], axis=1)
    bottom = jnp.concatenate([-im, re], axis=1)
    return jnp.concatenate([top, bottom], axis=0)


def kernel(
    g, s, w, cpl, pol, zout,
    gv, sv, cv, srhs, midv, ub, rb, own, zb, zr, ib, lb, db, lr, dr, a1, a2, br, bi,
    pb, pr, pg, wx, acc, z2b,
    ld, cld, wld, xs, xr, zs, zrs, es, er, ds_, dr_, ps, pr_, ws, wr, gs, gr_, z2s, z2r, pols, lcl,
):
    e = lax.axis_index("energy")
    c = lax.axis_index("cell")
    x = lax.div(c, NZ)
    z = lax.rem(c, NZ)

    def xof(dx):
        return lax.rem(x + dx, NX)

    def zof(dz):
        return lax.rem(z + dz, NZ)

    def cell_of(dx, dz):
        return xof(dx) * NZ + zof(dz)

    def rows_of(dx):
        return pl.ds(xof(dx) * NZ, NZ)

    s_load = pltpu.make_async_copy(s, sv, ld.at[4])
    s_load.start()
    c_load = pltpu.make_async_copy(cpl, cv, cld)
    c_load.start()
    g_load = {}
    for n, dx in enumerate((2, 1, 3, 0)):
        g_load[dx] = pltpu.make_async_copy(g.at[:, rows_of(dx)], gv.at[:, rows_of(dx)], ld.at[n])
        g_load[dx].start()
    w_load = pltpu.make_async_copy(w.at[:, rows_of(0)], wx.at[x], wld)
    w_load.start()

    barrier = pltpu.get_barrier_semaphore()

    @pl.loop(1, NE)
    def _(n):
        pl.semaphore_signal(
            barrier, inc=1, device_id={"energy": lax.rem(e + n, NE)}, device_id_type=MESH
        )

    for d in (1, 2, 3):
        pl.semaphore_signal(barrier, inc=1, device_id={"cell": cell_of(d, 0)}, device_id_type=MESH)
        pl.semaphore_signal(barrier, inc=1, device_id={"cell": cell_of(0, d)}, device_id_type=MESH)

    def to_cell(src, dst, ssem, rsem, dx, dz):
        copy = pltpu.make_async_remote_copy(
            src_ref=src, dst_ref=dst, send_sem=ssem, recv_sem=rsem,
            device_id={"cell": cell_of(dx, dz)}, device_id_type=MESH,
        )
        copy.start()
        return copy

    s_load.wait()
    c_load.wait()
    srhs[...] = stacked(sv[0], sv[1])

    def mids(dx):
        g_load[dx].wait()
        rows = rows_of(dx)
        left = jnp.concatenate(
            [gv[0, rows].reshape(NZ * ORB, ORB), gv[1, rows].reshape(NZ * ORB, ORB)], axis=1
        )
        mid = dot(left, srhs[...])
        for zi in range(NZ):
            weight = cv[xof(dx) * NZ + zi, c].astype(F32)
            midv[dx, zi] = (mid[zi * ORB : (zi + 1) * ORB] * weight).astype(BF16)

    def part(dx, zi):
        i = xof(dx) * NZ + zi
        return dot_t(midv[dx, zi], stacked(gv[0, i], gv[1, i]))

    x_sends = []

    def unit(step, zi):
        u = UNITS[step, zi]
        hop = 1 if (step, zi) in RIGHT else 3
        dest = 2 if step == "D" else hop
        term = part(dest, zi)
        re, im = term[:, :ORB], term[:, ORB:]
        if step == "C":
            d = UNITS["D", zi]
            pltpu.make_async_copy(rb.at[d], rb.at[d], xr.at[d]).wait()
            re = re + rb[d, 0].astype(F32)
            im = im + rb[d, 1].astype(F32)
        ub[u, 0] = re.astype(BF16)
        ub[u, 1] = im.astype(BF16)
        return u, hop

    def send(unit_hop):
        u, hop = unit_hop
        x_sends.append(to_cell(ub.at[u], rb.at[u], xs.at[u], xr.at[u], hop, 0))

    mids(2)
    first = [unit("D", 0), unit("D", 2)]
    pl.semaphore_wait(barrier, NE - 1 + 6)
    for item in first:
        send(item)
    mids(1)
    send(unit("N", 2))
    mids(3)
    send(unit("N", 0))
    send(unit("D", 1))
    send(unit("D", 3))
    send(unit("C", 0))
    send(unit("C", 2))
    send(unit("N", 3))
    send(unit("N", 1))

    def interleaved(re, im, out):
        ib[pl.ds(0, ORB, 2), :] = re
        ib[pl.ds(1, ORB, 2), :] = im
        out[...] = ib[...].reshape(NE, 8, ORB).astype(BF16)

    def spread(src, dst, ssem, rsem):
        dst[e] = src[e]
        for dz in (2, 1, 3, 0):

            @pl.loop(1 if dz == 0 else 0, 8)
            def _(n):
                low = lax.rem(lax.rem(e, 8) + n, 8)
                to = lax.rem(lax.div(e, 8) + dz, 4) * 8 + low
                pltpu.make_async_remote_copy(
                    src_ref=src.at[to], dst_ref=dst.at[e], send_sem=ssem, recv_sem=rsem,
                    device_id={"energy": to}, device_id_type=MESH,
                ).start()

    def arrived(buf, sem):
        part_of = buf.at[pl.ds(0, NE - 1)]
        pltpu.make_async_copy(part_of, part_of, sem).wait()

    g_load[0].wait()
    gr0 = gv[0, c].astype(F32)
    gi0 = gv[1, c].astype(F32)
    interleaved(gr0 - gr0.T, gi0 + gi0.T, db)
    spread(db, dr, ds_, dr_)

    send(unit("C", 1))
    send(unit("C", 3))

    w_sends = []
    for n, dx in enumerate((1, 3, 2)):
        w_sends.append(to_cell(w.at[:, rows_of(dx)], wx.at[x], ws.at[n], wr.at[n], dx, 0))

    rows = rows_of(0)
    left = jnp.concatenate(
        [gv[0, rows].reshape(NZ * ORB, ORB), gv[1, rows].reshape(NZ * ORB, ORB)], axis=1
    )
    mid = dot(left, srhs[...])
    for zi in range(NZ):
        weight = cv[x * NZ + zi, c].astype(F32)
        midv[0, zi] = (mid[zi * ORB : (zi + 1) * ORB] * weight).astype(BF16)
        own[zi] = part(0, zi)

    def x_arrived(u):
        pltpu.make_async_copy(rb.at[u], rb.at[u], xr.at[u]).wait()

    for zi in (0, 2, 1, 3):
        a = UNITS["C", zi]
        b = UNITS["N", zi]
        x_arrived(b)
        x_arrived(a)
        both = own[zi]
        re = both[:, :ORB] + rb[a, 0].astype(F32) + rb[b, 0].astype(F32)
        im = both[:, ORB:] + rb[a, 1].astype(F32) + rb[b, 1].astype(F32)
        own[zi] = jnp.concatenate([re, im], axis=1)
        zb[zi, 0] = re.astype(BF16)
        zb[zi, 1] = im.astype(BF16)

        @pl.when(zi != z)
        def _():
            pltpu.make_async_remote_copy(
                src_ref=zb.at[zi], dst_ref=zr.at[z], send_sem=zs, recv_sem=zrs.at[z],
                device_id={"cell": x * NZ + zi}, device_id_type=MESH,
            ).start()

    both = own[z]
    re, im = both[:, :ORB], both[:, ORB:]
    for dz in (1, 3, 2):
        n = zof(dz)
        pltpu.make_async_copy(zr.at[n], zr.at[n], zrs.at[n]).wait()
        re = re + zr[n, 0].astype(F32)
        im = im + zr[n, 1].astype(F32)

    interleaved(re, im, lb)
    spread(lb, lr, es, er)

    even = lax.rem(lax.broadcasted_iota(jnp.int32, (NE, 8, ORB), 1), 2) == 0

    def row_after(v):
        return pltpu.roll(v, 7, 1)

    def row_before(v):
        return pltpu.roll(v, 1, 1)

    a1[pl.ds(NE, NE)] = jnp.zeros((NE, 8, ORB), F32)
    a2[pl.ds(NE, NE)] = jnp.zeros((NE, 8, ORB), F32)
    arrived(dr, dr_)
    arrived(lr, er)
    low = lr[...].astype(F32)
    high = (low + dr[...].astype(F32)) * (1.0 / math.sqrt(NE))
    a1[pl.ds(0, NE)] = jnp.where(even, row_after(low), -row_before(low))
    a2[pl.ds(0, NE)] = -low
    br[...] = jnp.where(even, high, row_before(high))
    bi[...] = jnp.where(even, row_after(high), high)

    @pl.loop(0, NE)
    def _(shift):
        window = pl.ds(shift, NE)
        pb[shift] = jnp.sum(a1[window] * br[...] + a2[window] * bi[...], axis=0).astype(BF16)

    spread(pb, pr, ps, pr_)

    for n in range(3):
        pltpu.make_async_copy(wx.at[0], wx.at[0], wr.at[n]).wait()
    w_load.wait()

    arrived(pr, pr_)
    g_sends = []
    for n, dx in enumerate((2, 1, 3)):
        g_sends.append(to_cell(pr, pg.at[x], gs.at[n], gr_.at[n], dx, 0))
    pol_out = pltpu.make_async_copy(pr, pol, pols)
    pol_out.start()

    z_sends = []
    recv_of = {2: 0, 3: 1, 1: 2}
    for dx in (0, 1, 3, 2):
        j = xof(dx)
        if dx == 0:
            raw = pr[...]
        else:
            n = recv_of[dx]
            pltpu.make_async_copy(pg.at[j], pg.at[j], gr_.at[n]).wait()
            raw = pg[j]
        ib[...] = raw.astype(F32).reshape(2 * ORB, ORB)
        rhs = stacked(ib[pl.ds(0, ORB, 2), :].astype(BF16), ib[pl.ds(1, ORB, 2), :].astype(BF16))
        left = jnp.concatenate(
            [wx[j, 0].reshape(NZ * ORB, ORB), wx[j, 1].reshape(NZ * ORB, ORB)], axis=1
        )
        mid = dot(left, rhs)
        for zi in range(NZ):
            weight = cv[x * NZ + zi, j * NZ + z].astype(F32)
            midv[dx, zi] = (mid[zi * ORB : (zi + 1) * ORB] * weight).astype(BF16)
        for n, dz in enumerate((2, 1, 3, 0)):
            zi = zof(dz)
            term = dot_t(midv[dx, zi], stacked(wx[j, 0, zi], wx[j, 1, zi]))
            if dx == 0:
                acc[dz] = term
            elif dx != 2:
                acc[dz] += term
            else:
                term = term + acc[dz]
                z2b[dz, 0] = term[:, :ORB].astype(BF16)
                z2b[dz, 1] = term[:, ORB:].astype(BF16)
                if dz == 0:
                    local = pltpu.make_async_copy(z2b.at[0], zout.at[z], lcl)
                    local.start()
                else:
                    z_sends.append(to_cell(z2b.at[dz], zout.at[z], z2s.at[n], z2r.at[n], 0, dz))

    for copy in x_sends + w_sends + g_sends + z_sends:
        copy.wait_send()
    for buf, sem in ((lb, es), (db, ds_), (pb, ps)):
        arrived(buf, sem)
    three = zb.at[pl.ds(0, 3)]
    pltpu.make_async_copy(three, three, zs).wait()
    for n in range(3):
        pltpu.make_async_copy(zout.at[0], zout.at[0], z2r.at[n]).wait()
    pol_out.wait()
    local.wait()


def on_device(g, s, w, coupling):
    block = (2, ORB, ORB)
    dma = pltpu.SemaphoreType.DMA
    vm = pltpu.VMEM
    pol, parts = pl.pallas_call(
        kernel,
        out_shape=(
            jax.ShapeDtypeStruct((NE, 8, ORB), BF16),
            jax.ShapeDtypeStruct((NZ, *block), BF16),
        ),
        in_specs=[pl.BlockSpec(memory_space=pl.ANY)] * 4,
        out_specs=(pl.BlockSpec(memory_space=pl.ANY), pl.BlockSpec(memory_space=pl.ANY)),
        scratch_shapes=[
            vm((2, NX * NZ, ORB, ORB), BF16),
            vm(block, BF16),
            pltpu.SMEM((NX * NZ, NX * NZ), jnp.int32),
            vm((2 * ORB, 2 * ORB), BF16),
            vm((NX, NZ, ORB, 2 * ORB), BF16),
            vm((12, *block), BF16),
            vm((12, *block), BF16),
            vm((NZ, ORB, 2 * ORB), F32),
            vm((NZ, *block), BF16),
            vm((NZ, *block), BF16),
            vm((2 * ORB, ORB), F32),
            vm((NE, 8, ORB), BF16),
            vm((NE, 8, ORB), BF16),
            vm((NE, 8, ORB), BF16),
            vm((NE, 8, ORB), BF16),
            vm((2 * NE, 8, ORB), F32),
            vm((2 * NE, 8, ORB), F32),
            vm((NE, 8, ORB), F32),
            vm((NE, 8, ORB), F32),
            vm((NE, 8, ORB), BF16),
            vm((NE, 8, ORB), BF16),
            vm((NX, NE, 8, ORB), BF16),
            vm((NX, 2, NZ, ORB, ORB), BF16),
            vm((NZ, ORB, 2 * ORB), F32),
            vm((NZ, *block), BF16),
            dma((5,)),
            dma,
            dma,
            dma((12,)),
            dma((12,)),
            dma,
            dma((NZ,)),
            dma,
            dma,
            dma,
            dma,
            dma,
            dma,
            dma((3,)),
            dma((3,)),
            dma((3,)),
            dma((3,)),
            dma((3,)),
            dma((3,)),
            dma,
            dma,
        ],
        compiler_params=pltpu.CompilerParams(collective_id=0, has_side_effects=True),
    )(g.reshape(2, NX * NZ, ORB, ORB), s.reshape(block), w.reshape(2, NX * NZ, ORB, ORB), coupling)
    polar = jnp.transpose(pol.reshape(ORB, 2, ORB), (1, 0, 2)).reshape(1, 2, 1, ORB * ORB)
    screened = parts.astype(F32).sum(axis=0).astype(BF16)
    return polar, screened.reshape(1, 2, 1, ORB, ORB)


def solution(mesh):
    return jax.shard_map(
        on_device,
        mesh=mesh,
        in_specs=(
            P(None, "energy", None, None, "cell"),
            P(None, "energy", None, "cell"),
            P(None, "energy", None, None, "cell"),
            P(),
        ),
        out_specs=(P("cell", None, "energy", None), P("cell", None, "energy", None, None)),
        check_vma=False,
    )
```

time: 143 us -> 70.8 us (0.50)
  Pallas kernels: 0 us -> 67.7 us
  blocking collectives: 56 us -> 0 us
  waiting for transfers between devices: 53.9 us -> 0 us
  matrix products: 13.5 us -> 0 us
  starting transfers between devices: 12.7 us -> 0 us
  local copies, waits for them, and re-layouts: 4.2 us -> 0.63 us
    pallas_call x0 -> x1, Pallas kernels: none -> 67.7 us  [on_device(): pl.pallas_call(kernel, out_shape=(jax.ShapeDtypeStruct((NE, 8, ORB), BF16...]
    all_to_all x3 -> x0, blocking collectives: 56 us -> none  [the longest x2 33.9 us: moved_by_axis(): out = lax.all_to_all(out, axes[k], k, k, tiled=True)]
    all_to_all x2 -> x0, waiting for transfers between devices: 53.9 us -> none  [sent_and_summed(): lax.all_to_all(parts, axis, split_axis=0, concat_axis=0, tiled=True)]
    dot_general x36 -> x0, matrix products: 13.5 us -> none  [the longest x8 4.15 us: adjoint_product(): jnp.einsum('eibjc,eidjc->iebd', left, right, preferred_element_type=jnp.f...]
    all_to_all x2 -> x0, starting transfers between devices: 12.7 us -> none  [sent_and_summed(): lax.all_to_all(parts, axis, split_axis=0, concat_axis=0, tiled=True)]
    another operation x7 -> x0, local copies, waits for them, and re-layouts: 2.28 us -> none  [the longest x2 2.12 us: sandwich_rows(): return jnp.stack([part_re, part_im], axis=1)]
  transfers between devices with their start and end apart: 2 -> 0, of which waited for: 2 -> 0; matrix products, arithmetic and copies ran while one was open for 0% -> 0% of each run, Pallas kernels for 0% -> 0%
where the time goes in v1:
time: 70.8 us; the launch traced here: 70.7 us
  Pallas kernels  67.7 us (96%)
  other arithmetic  1.67 us (2%)
    pallas_call x1, Pallas kernels, on_device(): pl.pallas_call(kernel, out_shape=(jax.ShapeDtypeStruct((NE, 8, ORB), BF16...  67.7 us
    reduce_sum x1, other arithmetic, on_device(): screened = parts.astype(F32).sum(axis=0).astype(BF16)  1.67 us

profile of v1, /device:TPU:1, one launch (start us, length us, event | category | flops | bytes accessed | tf_op | source)
XLA Modules:
  0.0 70.7 jit_solution(385379187198169351)
XLA Ops:
  0.6 67.7 %shard_map.59 = (bf16[32,8,128]{2,1,0:T(8,128)(2,1)}, bf16[4,2,128,128]{3,2,1,0:T(8,128)(2,1)}) custom-call(bf16[2,16,128,128]{3,2,1,0:T(8,128)(2,1)} %bitcast.9, bf16[2,128,128]{2,1,0:T(8,128)(2,1)} %bitcast.11, bf16[2,16,128,128]{3,2,1,0:T(8,128)(2,1)} %bitcast.10, s32[16,16]{1,0:T(8,128)} %cpl.1), custom_call_target="tpu_custom_call" | custom-call | tf_op jit(solution)/shard_map/pallas_call | solution.py:314
  68.4 0.0 copy-start
  68.4 1.7 %reduce_sum.12 = bf16[2,128,128]{2,1,0:T(8,128)(2,1)} reduce(bf16[4,2,128,128]{3,2,1,0:T(8,128)(2,1)} %get-tuple-element.5, bf16[]{:T(256)} %constant.2.clone.1), dimensions={0}, to_apply=%region_0.0 | reduce | flops 98304 | bytes 327682 | tf_op jit(solution)/shard_map/reduce_sum | solution.py:373
  70.0 0.0 copy-done
  70.0 0.6 copy.8
Async XLA Ops:
  68.4 1.7 %copy-start = (bf16[32,8,128]{2,1,0:T(8,128)(2,1)S(1)}, bf16[32,8,128]{2,1,0:T(8,128)(2,1)}, u32[]{:S(2)}) copy-start(bf16[32,8,128]{2,1,0:T(8,128)(2,1)} %get-tuple-element.4) | copy-start | bytes 196612

commit v2 on v1

--- a/solution.py
+++ b/solution.py
@@ -38,7 +38,7 @@
     g, s, w, cpl, pol, zout,
     gv, sv, cv, srhs, midv, ub, rb, own, zb, zr, ib, lb, db, lr, dr, a1, a2, br, bi,
     pb, pr, pg, wx, acc, z2b,
-    ld, cld, wld, xs, xr, zs, zrs, es, er, ds_, dr_, ps, pr_, ws, wr, gs, gr_, z2s, z2r, pols, lcl,
+    ld, cld, wld, xs, xr, zs, zrs, es, er, ds_, dr_, ps, pr_, f1, f2, ws, wr, gs, gr_, z2s, z2r, pols, lcl,
 ):
     e = lax.axis_index("energy")
     c = lax.axis_index("cell")
@@ -70,12 +70,20 @@
 
     barrier = pltpu.get_barrier_semaphore()
 
-    @pl.loop(1, NE)
+    plane = lax.div(e, 8) * 8
+
+    @pl.loop(1, 8)
     def _(n):
-        pl.semaphore_signal(
-            barrier, inc=1, device_id={"energy": lax.rem(e + n, NE)}, device_id_type=MESH
-        )
-
+        mate = plane + lax.rem(e + n, 8)
+        pl.semaphore_signal(barrier, inc=1, device_id={"energy": mate}, device_id_type=MESH)
+
+    def greet_along_z(sem):
+        for d in (8, NE - 8):
+            pl.semaphore_signal(
+                sem, inc=1, device_id={"energy": lax.rem(e + d, NE)}, device_id_type=MESH
+            )
+
+    greet_along_z(barrier)
     for d in (1, 2, 3):
         pl.semaphore_signal(barrier, inc=1, device_id={"cell": cell_of(d, 0)}, device_id_type=MESH)
         pl.semaphore_signal(barrier, inc=1, device_id={"cell": cell_of(0, d)}, device_id_type=MESH)
@@ -130,7 +138,8 @@
 
     mids(2)
     first = [unit("D", 0), unit("D", 2)]
-    pl.semaphore_wait(barrier, NE - 1 + 6)
+    pl.semaphore_wait(barrier, 7 + 2 + 6)
+    greet_along_z(f1)
     for item in first:
         send(item)
     mids(1)
@@ -149,18 +158,19 @@
         ib[pl.ds(1, ORB, 2), :] = im
         out[...] = ib[...].reshape(NE, 8, ORB).astype(BF16)
 
+    def send_plane(src, dst, ssem, rsem, dz):
+        @pl.loop(1 if dz == 0 else 0, 8)
+        def _(n):
+            to = lax.rem(plane + 8 * dz, NE) + lax.rem(e + n, 8)
+            pltpu.make_async_remote_copy(
+                src_ref=src.at[to], dst_ref=dst.at[e], send_sem=ssem, recv_sem=rsem,
+                device_id={"energy": to}, device_id_type=MESH,
+            ).start()
+
     def spread(src, dst, ssem, rsem):
         dst[e] = src[e]
         for dz in (2, 1, 3, 0):
-
-            @pl.loop(1 if dz == 0 else 0, 8)
-            def _(n):
-                low = lax.rem(lax.rem(e, 8) + n, 8)
-                to = lax.rem(lax.div(e, 8) + dz, 4) * 8 + low
-                pltpu.make_async_remote_copy(
-                    src_ref=src.at[to], dst_ref=dst.at[e], send_sem=ssem, recv_sem=rsem,
-                    device_id={"energy": to}, device_id_type=MESH,
-                ).start()
+            send_plane(src, dst, ssem, rsem, dz)
 
     def arrived(buf, sem):
         part_of = buf.at[pl.ds(0, NE - 1)]
@@ -170,7 +180,8 @@
     gr0 = gv[0, c].astype(F32)
     gi0 = gv[1, c].astype(F32)
     interleaved(gr0 - gr0.T, gi0 + gi0.T, db)
-    spread(db, dr, ds_, dr_)
+    pl.semaphore_wait(f1, 2)
+    greet_along_z(f2)
 
     send(unit("C", 1))
     send(unit("C", 3))
@@ -188,6 +199,9 @@
         weight = cv[x * NZ + zi, c].astype(F32)
         midv[0, zi] = (mid[zi * ORB : (zi + 1) * ORB] * weight).astype(BF16)
         own[zi] = part(0, zi)
+
+    pl.semaphore_wait(f2, 2)
+    spread(db, dr, ds_, dr_)
 
     def x_arrived(u):
         pltpu.make_async_copy(rb.at[u], rb.at[u], xr.at[u]).wait()
@@ -230,8 +244,8 @@
     def row_before(v):
         return pltpu.roll(v, 1, 1)
 
-    a1[pl.ds(NE, NE)] = jnp.zeros((NE, 8, ORB), F32)
-    a2[pl.ds(NE, NE)] = jnp.zeros((NE, 8, ORB), F32)
+    a1[pl.ds(NE, 8)] = jnp.zeros((8, 8, ORB), F32)
+    a2[pl.ds(NE, 8)] = jnp.zeros((8, 8, ORB), F32)
     arrived(dr, dr_)
     arrived(lr, er)
     low = lr[...].astype(F32)
@@ -241,21 +255,33 @@
     br[...] = jnp.where(even, high, row_before(high))
     bi[...] = jnp.where(even, row_after(high), high)
 
-    @pl.loop(0, NE)
-    def _(shift):
-        window = pl.ds(shift, NE)
-        pb[shift] = jnp.sum(a1[window] * br[...] + a2[window] * bi[...], axis=0).astype(BF16)
-
-    spread(pb, pr, ps, pr_)
+    for dz in (2, 1, 3, 0):
+        first = lax.rem(plane + 8 * dz, NE)
+
+        def eight(block, total, first=first):
+            for n in range(8):
+                at = block * 8 + n
+                window = pl.ds(first + at, 8)
+                total = total + a1[window] * br[at] + a2[window] * bi[at]
+            return total
+
+        total = lax.fori_loop(0, lax.div(NE - first, 8), eight, jnp.zeros((8, 8, ORB), F32))
+        pb[pl.ds(first, 8)] = total.astype(BF16)
+        if dz == 0:
+            pr[e] = pb[e]
+        send_plane(pb, pr, ps, pr_.at[dz], dz)
 
     for n in range(3):
         pltpu.make_async_copy(wx.at[0], wx.at[0], wr.at[n]).wait()
     w_load.wait()
 
-    arrived(pr, pr_)
     g_sends = []
-    for n, dx in enumerate((2, 1, 3)):
-        g_sends.append(to_cell(pr, pg.at[x], gs.at[n], gr_.at[n], dx, 0))
+    for dz in (0, 1, 3, 2):
+        tiles = pl.ds(lax.rem(plane + (NE - 8 * dz), NE), 8)
+        came = pr.at[pl.ds(0, 7 if dz == 0 else 8)]
+        pltpu.make_async_copy(came, came, pr_.at[dz]).wait()
+        for n, dx in enumerate((2, 1, 3)):
+            g_sends.append(to_cell(pr.at[tiles], pg.at[x, tiles], gs.at[n], gr_.at[n], dx, 0))
     pol_out = pltpu.make_async_copy(pr, pol, pols)
     pol_out.start()
 
@@ -278,8 +304,8 @@
         for zi in range(NZ):
             weight = cv[x * NZ + zi, j * NZ + z].astype(F32)
             midv[dx, zi] = (mid[zi * ORB : (zi + 1) * ORB] * weight).astype(BF16)
-        for n, dz in enumerate((2, 1, 3, 0)):
-            zi = zof(dz)
+        for n, dz in enumerate((2, 3, 1, 0)):
+            zi = lax.bitwise_xor(z, dz)
             term = dot_t(midv[dx, zi], stacked(wx[j, 0, zi], wx[j, 1, zi]))
             if dx == 0:
                 acc[dz] = term
@@ -293,7 +319,12 @@
                     local = pltpu.make_async_copy(z2b.at[0], zout.at[z], lcl)
                     local.start()
                 else:
-                    z_sends.append(to_cell(z2b.at[dz], zout.at[z], z2s.at[n], z2r.at[n], 0, dz))
+                    copy = pltpu.make_async_remote_copy(
+                        src_ref=z2b.at[dz], dst_ref=zout.at[z], send_sem=z2s.at[n], recv_sem=z2r.at[n],
+                        device_id={"cell": x * NZ + zi}, device_id_type=MESH,
+                    )
+                    copy.start()
+                    z_sends.append(copy)
 
     for copy in x_sends + w_sends + g_sends + z_sends:
         copy.wait_send()
@@ -335,8 +366,8 @@
             vm((NE, 8, ORB), BF16),
             vm((NE, 8, ORB), BF16),
             vm((NE, 8, ORB), BF16),
-            vm((2 * NE, 8, ORB), F32),
-            vm((2 * NE, 8, ORB), F32),
+            vm((NE + 8, 8, ORB), F32),
+            vm((NE + 8, 8, ORB), F32),
             vm((NE, 8, ORB), F32),
             vm((NE, 8, ORB), F32),
             vm((NE, 8, ORB), BF16),
@@ -357,7 +388,9 @@
             dma,
             dma,
             dma,
-            dma,
+            dma((4,)),
+            pltpu.SemaphoreType.REGULAR,
+            pltpu.SemaphoreType.REGULAR,
             dma((3,)),
             dma((3,)),
             dma((3,)),
@@ -370,7 +403,7 @@
         compiler_params=pltpu.CompilerParams(collective_id=0, has_side_effects=True),
     )(g.reshape(2, NX * NZ, ORB, ORB), s.reshape(block), w.reshape(2, NX * NZ, ORB, ORB), coupling)
     polar = jnp.transpose(pol.reshape(ORB, 2, ORB), (1, 0, 2)).reshape(1, 2, 1, ORB * ORB)
-    screened = parts.astype(F32).sum(axis=0).astype(BF16)
+    screened = sum(parts[n].astype(F32) for n in range(NZ)).astype(BF16)
     return polar, screened.reshape(1, 2, 1, ORB, ORB)
 
 

time: 70.8 us -> 63.3 us (0.89)
  the two profiles are of different devices: /device:TPU:1 before, /device:TPU:6 now
where the time goes in v2:
time: 63.3 us; the launch traced here: 63.1 us
  Pallas kernels  60.2 us (95%)
  other arithmetic  1.63 us (3%)
  between operations  0.65 us (1%)
    pallas_call x1, Pallas kernels, on_device(): pl.pallas_call(kernel, out_shape=(jax.ShapeDtypeStruct((NE, 8, ORB), BF16...  60.2 us
    unnamed x1, other arithmetic  1.63 us

profile of v2, /device:TPU:6, one launch (start us, length us, event | category | flops | bytes accessed | tf_op | source)
XLA Modules:
  0.0 63.1 jit_solution(13382694203715396745)
XLA Ops:
  0.6 60.2 %shard_map.59 = (bf16[32,8,128]{2,1,0:T(8,128)(2,1)}, bf16[4,2,128,128]{3,2,1,0:T(8,128)(2,1)}) custom-call(bf16[2,16,128,128]{3,2,1,0:T(8,128)(2,1)} %bitcast.12, bf16[2,128,128]{2,1,0:T(8,128)(2,1)} %bitcast.14, bf16[2,16,128,128]{3,2,1,0:T(8,128)(2,1)} %bitcast.13, s32[16,16]{1,0:T(8,128)} %cpl.1), custom_call_target="tpu_custom_call" | custom-call | tf_op jit(solution)/shard_map/pallas_call | solution.py:345
  60.8 0.0 copy-start
  60.8 1.6 %fusion = bf16[1,2,1,128,128]{4,3,2,1,0:T(8,128)(2,1)} fusion(bf16[4,2,128,128]{3,2,1,0:T(8,128)(2,1)} %get-tuple-element.5), kind=kLoop, calls=%fused_computation.1 | loop fusion | flops 262144 | bytes 327680
  62.5 0.0 copy-done
  62.5 0.6 copy.9
Async XLA Ops:
  60.8 1.6 %copy-start = (bf16[32,8,128]{2,1,0:T(8,128)(2,1)S(1)}, bf16[32,8,128]{2,1,0:T(8,128)(2,1)}, u32[]{:S(2)}) copy-start(bf16[32,8,128]{2,1,0:T(8,128)(2,1)} %get-tuple-element.4) | copy-start | bytes 196612

commit v3 on v2

--- a/solution.py
+++ b/solution.py
@@ -14,6 +14,7 @@
 F32 = jnp.float32
 BF16 = jnp.bfloat16
 MESH = pl.DeviceIdType.MESH
+VL = 16 * 1024 * 1024
 
 RIGHT = {("D", 0): 0, ("D", 1): 1, ("N", 2): 2, ("N", 3): 3, ("C", 0): 4, ("C", 1): 5}
 LEFT = {("D", 2): 6, ("D", 3): 7, ("N", 0): 8, ("N", 1): 9, ("C", 2): 10, ("C", 3): 11}
@@ -36,9 +37,9 @@
 
 def kernel(
     g, s, w, cpl, pol, zout,
-    gv, sv, cv, srhs, midv, ub, rb, own, zb, zr, ib, lb, db, lr, dr, a1, a2, br, bi,
+    gv, sv, cv, srhs, midv, ub, rb, own, zb, zr, ib, lb, db, lr, a1, a2, br, bi,
     pb, pr, pg, wx, acc, z2b,
-    ld, cld, wld, xs, xr, zs, zrs, es, er, ds_, dr_, ps, pr_, f1, f2, ws, wr, gs, gr_, z2s, z2r, pols, lcl,
+    ld, cld, wld, xs, xr, zs, zrs, es, er, ps, pr_, fr, f1, f2, ws, wr, gs, gr_, z2s, z2r, pols, lcl,
 ):
     e = lax.axis_index("energy")
     c = lax.axis_index("cell")
@@ -71,11 +72,20 @@
     barrier = pltpu.get_barrier_semaphore()
 
     plane = lax.div(e, 8) * 8
-
-    @pl.loop(1, 8)
-    def _(n):
-        mate = plane + lax.rem(e + n, 8)
-        pl.semaphore_signal(barrier, inc=1, device_id={"energy": mate}, device_id_type=MESH)
+    seat = lax.rem(e, 8)
+
+    def greet(sem):
+        for d in (1, NX - 1):
+            pl.semaphore_signal(sem, inc=1, device_id={"cell": cell_of(d, 0)}, device_id_type=MESH)
+        for d in (2, 6):
+            to = plane + lax.rem(seat + d, 8)
+            pl.semaphore_signal(sem, inc=1, device_id={"energy": to}, device_id_type=MESH)
+        mate = lax.bitwise_xor(e, 1)
+        pl.semaphore_signal(sem, inc=1, device_id={"energy": mate}, device_id_type=MESH)
+        for d in (1, 15):
+            at = lax.rem(lax.div(e, 8) * NZ + z + d, 16)
+            to = {"energy": lax.div(at, NZ) * 8 + seat, "cell": x * NZ + lax.rem(at, NZ)}
+            pl.semaphore_signal(sem, inc=1, device_id=to, device_id_type=MESH)
 
     def greet_along_z(sem):
         for d in (8, NE - 8):
@@ -83,10 +93,10 @@
                 sem, inc=1, device_id={"energy": lax.rem(e + d, NE)}, device_id_type=MESH
             )
 
-    greet_along_z(barrier)
-    for d in (1, 2, 3):
-        pl.semaphore_signal(barrier, inc=1, device_id={"cell": cell_of(d, 0)}, device_id_type=MESH)
-        pl.semaphore_signal(barrier, inc=1, device_id={"cell": cell_of(0, d)}, device_id_type=MESH)
+    def heard(sem, count):
+        pl.semaphore_wait(sem, count)
+
+    greet(barrier)
 
     def to_cell(src, dst, ssem, rsem, dx, dz):
         copy = pltpu.make_async_remote_copy(
@@ -138,25 +148,30 @@
 
     mids(2)
     first = [unit("D", 0), unit("D", 2)]
-    pl.semaphore_wait(barrier, 7 + 2 + 6)
-    greet_along_z(f1)
+    heard(barrier, 7)
+    greet(fr.at[0])
     for item in first:
         send(item)
     mids(1)
     send(unit("N", 2))
     mids(3)
     send(unit("N", 0))
+    heard(fr.at[0], 7)
+    greet(fr.at[1])
     send(unit("D", 1))
     send(unit("D", 3))
+    heard(fr.at[1], 7)
+    greet(fr.at[2])
     send(unit("C", 0))
     send(unit("C", 2))
     send(unit("N", 3))
     send(unit("N", 1))
+    heard(fr.at[2], 7)
+    greet_along_z(f1)
 
     def interleaved(re, im, out):
-        ib[pl.ds(0, ORB, 2), :] = re
-        ib[pl.ds(1, ORB, 2), :] = im
-        out[...] = ib[...].reshape(NE, 8, ORB).astype(BF16)
+        out[pl.ds(0, ORB, 2), :] = re
+        out[pl.ds(1, ORB, 2), :] = im
 
     def send_plane(src, dst, ssem, rsem, dz):
         @pl.loop(1 if dz == 0 else 0, 8)
@@ -167,41 +182,25 @@
                 device_id={"energy": to}, device_id_type=MESH,
             ).start()
 
-    def spread(src, dst, ssem, rsem):
-        dst[e] = src[e]
-        for dz in (2, 1, 3, 0):
-            send_plane(src, dst, ssem, rsem, dz)
-
     def arrived(buf, sem):
         part_of = buf.at[pl.ds(0, NE - 1)]
         pltpu.make_async_copy(part_of, part_of, sem).wait()
 
-    g_load[0].wait()
+    send(unit("C", 1))
+    send(unit("C", 3))
+
+    w_sends = []
+    for n, dx in enumerate((1, 3, 2)):
+        w_sends.append(to_cell(w.at[:, rows_of(dx)], wx.at[x], ws.at[n], wr.at[n], dx, 0))
+
+    mids(0)
+    for zi in range(NZ):
+        own[zi] = part(0, zi)
     gr0 = gv[0, c].astype(F32)
     gi0 = gv[1, c].astype(F32)
     interleaved(gr0 - gr0.T, gi0 + gi0.T, db)
-    pl.semaphore_wait(f1, 2)
+    heard(f1, 2)
     greet_along_z(f2)
-
-    send(unit("C", 1))
-    send(unit("C", 3))
-
-    w_sends = []
-    for n, dx in enumerate((1, 3, 2)):
-        w_sends.append(to_cell(w.at[:, rows_of(dx)], wx.at[x], ws.at[n], wr.at[n], dx, 0))
-
-    rows = rows_of(0)
-    left = jnp.concatenate(
-        [gv[0, rows].reshape(NZ * ORB, ORB), gv[1, rows].reshape(NZ * ORB, ORB)], axis=1
-    )
-    mid = dot(left, srhs[...])
-    for zi in range(NZ):
-        weight = cv[x * NZ + zi, c].astype(F32)
-        midv[0, zi] = (mid[zi * ORB : (zi + 1) * ORB] * weight).astype(BF16)
-        own[zi] = part(0, zi)
-
-    pl.semaphore_wait(f2, 2)
-    spread(db, dr, ds_, dr_)
 
     def x_arrived(u):
         pltpu.make_async_copy(rb.at[u], rb.at[u], xr.at[u]).wait()
@@ -233,8 +232,13 @@
         re = re + zr[n, 0].astype(F32)
         im = im + zr[n, 1].astype(F32)
 
-    interleaved(re, im, lb)
-    spread(lb, lr, es, er)
+    interleaved(re, im, ib)
+    lb[:, 0] = ib[...].reshape(NE, 8, ORB).astype(BF16)
+    lb[:, 1] = (ib[...] + db[...]).reshape(NE, 8, ORB).astype(BF16)
+    heard(f2, 2)
+    lr[e] = lb[e]
+    for dz in (2, 1, 3, 0):
+        send_plane(lb, lr, es, er, dz)
 
     even = lax.rem(lax.broadcasted_iota(jnp.int32, (NE, 8, ORB), 1), 2) == 0
 
@@ -246,10 +250,9 @@
 
     a1[pl.ds(NE, 8)] = jnp.zeros((8, 8, ORB), F32)
     a2[pl.ds(NE, 8)] = jnp.zeros((8, 8, ORB), F32)
-    arrived(dr, dr_)
     arrived(lr, er)
-    low = lr[...].astype(F32)
-    high = (low + dr[...].astype(F32)) * (1.0 / math.sqrt(NE))
+    low = lr[:, 0].astype(F32)
+    high = lr[:, 1].astype(F32) * (1.0 / math.sqrt(NE))
     a1[pl.ds(0, NE)] = jnp.where(even, row_after(low), -row_before(low))
     a2[pl.ds(0, NE)] = -low
     br[...] = jnp.where(even, high, row_before(high))
@@ -328,7 +331,7 @@
 
     for copy in x_sends + w_sends + g_sends + z_sends:
         copy.wait_send()
-    for buf, sem in ((lb, es), (db, ds_), (pb, ps)):
+    for buf, sem in ((lb, es), (pb, ps)):
         arrived(buf, sem)
     three = zb.at[pl.ds(0, 3)]
     pltpu.make_async_copy(three, three, zs).wait()
@@ -342,13 +345,16 @@
     block = (2, ORB, ORB)
     dma = pltpu.SemaphoreType.DMA
     vm = pltpu.VMEM
+    operands = (
+        g.reshape(2, NX * NZ, ORB, ORB), s.reshape(block), w.reshape(2, NX * NZ, ORB, ORB), coupling
+    )
     pol, parts = pl.pallas_call(
         kernel,
         out_shape=(
             jax.ShapeDtypeStruct((NE, 8, ORB), BF16),
             jax.ShapeDtypeStruct((NZ, *block), BF16),
         ),
-        in_specs=[pl.BlockSpec(memory_space=pl.ANY)] * 4,
+        in_specs=[pl.BlockSpec(memory_space=pltpu.HBM)] * 4,
         out_specs=(pl.BlockSpec(memory_space=pl.ANY), pl.BlockSpec(memory_space=pl.ANY)),
         scratch_shapes=[
             vm((2, NX * NZ, ORB, ORB), BF16),
@@ -362,10 +368,9 @@
             vm((NZ, *block), BF16),
             vm((NZ, *block), BF16),
             vm((2 * ORB, ORB), F32),
-            vm((NE, 8, ORB), BF16),
-            vm((NE, 8, ORB), BF16),
-            vm((NE, 8, ORB), BF16),
-            vm((NE, 8, ORB), BF16),
+            vm((NE, 2, 8, ORB), BF16),
+            vm((2 * ORB, ORB), F32),
+            vm((NE, 2, 8, ORB), BF16),
             vm((NE + 8, 8, ORB), F32),
             vm((NE + 8, 8, ORB), F32),
             vm((NE, 8, ORB), F32),
@@ -386,9 +391,8 @@
             dma,
             dma,
             dma,
-            dma,
-            dma,
             dma((4,)),
+            pltpu.SemaphoreType.REGULAR((3,)),
             pltpu.SemaphoreType.REGULAR,
             pltpu.SemaphoreType.REGULAR,
             dma((3,)),
@@ -400,8 +404,8 @@
             dma,
             dma,
         ],
-        compiler_params=pltpu.CompilerParams(collective_id=0, has_side_effects=True),
-    )(g.reshape(2, NX * NZ, ORB, ORB), s.reshape(block), w.reshape(2, NX * NZ, ORB, ORB), coupling)
+        compiler_params=pltpu.CompilerParams(collective_id=0, has_side_effects=True, vmem_limit_bytes=VL),
+    )(*(pltpu.with_memory_space_constraint(v, pltpu.HBM) for v in operands))
     polar = jnp.transpose(pol.reshape(ORB, 2, ORB), (1, 0, 2)).reshape(1, 2, 1, ORB * ORB)
     screened = sum(parts[n].astype(F32) for n in range(NZ)).astype(BF16)
     return polar, screened.reshape(1, 2, 1, ORB, ORB)

time: 63.3 us -> 60.7 us (0.959)
  Pallas kernels: 60.2 us -> 58.7 us
  other arithmetic: 1.63 us -> 0.67 us
    pallas_call x1, Pallas kernels: 60.2 us -> 58.7 us  [on_device(): pl.pallas_call(kernel, out_shape=(jax.ShapeDtypeStruct((NE, 8, ORB), BF16...]
    unnamed x1, other arithmetic: 1.63 us -> 0.67 us
where the time goes in v3:
time: 60.7 us; the launch traced here: 60.6 us
  Pallas kernels  58.7 us (97%)
  other arithmetic  0.67 us (1%)
  between operations  0.64 us (1%)
  local copies, waits for them, and re-layouts  0.63 us (1%)
    pallas_call x1, Pallas kernels, on_device(): pl.pallas_call(kernel, out_shape=(jax.ShapeDtypeStruct((NE, 8, ORB), BF16...  58.7 us

profile of v3, /device:TPU:6, one launch (start us, length us, event | category | flops | bytes accessed | tf_op | source)
XLA Modules:
  0.0 60.6 jit_solution(7100006450186601798)
XLA Ops:
  0.6 58.7 %shard_map.59 = (bf16[32,8,128]{2,1,0:T(8,128)(2,1)S(1)}, bf16[4,2,128,128]{3,2,1,0:T(8,128)(2,1)S(1)}) custom-call(bf16[2,16,128,128]{3,2,1,0:T(8,128)(2,1)} %bitcast.13, bf16[2,128,128]{2,1,0:T(8,128)(2,1)} %bitcast.15, bf16[2,16,128,128]{3,2,1,0:T(8,128)(2,1)} %bitcast.14, s32[16,16]{1,0:T(8,128)} %cpl.1), custom_call_target="tpu_custom_call" | custom-call | tf_op jit(solution)/shard_map/pallas_call | solution.py:351
  59.3 0.7 %fusion = bf16[1,2,1,128,128]{4,3,2,1,0:T(8,128)(2,1)} fusion(bf16[4,2,128,128]{3,2,1,0:T(8,128)(2,1)S(1)} %get-tuple-element.5), kind=kLoop, calls=%fused_computation.1 | loop fusion | flops 262144 | bytes 327680
  60.0 0.6 %copy.9 = bf16[1,2,1,16384]{3,1,2,0:T(2,128)(2,1)} copy(bf16[1,2,1,16384]{3,1,2,0:T(2,128)(2,1)S(1)} %bitcast.12) | data formatting | bytes 131072

commit v4 on v3

--- a/solution.py
+++ b/solution.py
@@ -16,9 +16,11 @@
 MESH = pl.DeviceIdType.MESH
 VL = 16 * 1024 * 1024
 
-RIGHT = {("D", 0): 0, ("D", 1): 1, ("N", 2): 2, ("N", 3): 3, ("C", 0): 4, ("C", 1): 5}
-LEFT = {("D", 2): 6, ("D", 3): 7, ("N", 0): 8, ("N", 1): 9, ("C", 2): 10, ("C", 3): 11}
-UNITS = {**RIGHT, **LEFT}
+ROWS = ORB // 4
+
+RD, RC, RN = (0, 1), (2, 1), (4, 1)
+LD, LN, LC = (6, 3), (8, 3), (10, 3)
+ORDER = (2, 1, 3, 0)
 
 
 def dot(a, b):
@@ -37,7 +39,7 @@
 
 def kernel(
     g, s, w, cpl, pol, zout,
-    gv, sv, cv, srhs, midv, ub, rb, own, zb, zr, ib, lb, db, lr, a1, a2, br, bi,
+    gv, sv, cv, srhs, midv, ub, rb, own, zb, zr, ib, il, lb, db, lr, a1, a2, br, bi,
     pb, pr, pg, wx, acc, z2b,
     ld, cld, wld, xs, xr, zs, zrs, es, er, ps, pr_, fr, f1, f2, ws, wr, gs, gr_, z2s, z2r, pols, lcl,
 ):
@@ -125,53 +127,53 @@
         i = xof(dx) * NZ + zi
         return dot_t(midv[dx, zi], stacked(gv[0, i], gv[1, i]))
 
+    def split(term, out, at, dtype):
+        for q in range(4):
+            out[q, at, 0] = term[q * ROWS : (q + 1) * ROWS, :ORB].astype(dtype)
+            out[q, at, 1] = term[q * ROWS : (q + 1) * ROWS, ORB:].astype(dtype)
+
+    def terms(pair, dest, block):
+        for n in range(2):
+            split(part(dest, block + n), ub, pair[0] + n, BF16)
+
+    def quarter(t):
+        return lax.rem(lax.div(e, 8) + ORDER[t], 4)
+
     x_sends = []
 
-    def unit(step, zi):
-        u = UNITS[step, zi]
-        hop = 1 if (step, zi) in RIGHT else 3
-        dest = 2 if step == "D" else hop
-        term = part(dest, zi)
-        re, im = term[:, :ORB], term[:, ORB:]
-        if step == "C":
-            d = UNITS["D", zi]
-            pltpu.make_async_copy(rb.at[d], rb.at[d], xr.at[d]).wait()
-            re = re + rb[d, 0].astype(F32)
-            im = im + rb[d, 1].astype(F32)
-        ub[u, 0] = re.astype(BF16)
-        ub[u, 1] = im.astype(BF16)
-        return u, hop
-
-    def send(unit_hop):
-        u, hop = unit_hop
-        x_sends.append(to_cell(ub.at[u], rb.at[u], xs.at[u], xr.at[u], hop, 0))
-
-    mids(2)
-    first = [unit("D", 0), unit("D", 2)]
-    heard(barrier, 7)
-    greet(fr.at[0])
-    for item in first:
-        send(item)
-    mids(1)
-    send(unit("N", 2))
-    mids(3)
-    send(unit("N", 0))
-    heard(fr.at[0], 7)
-    greet(fr.at[1])
-    send(unit("D", 1))
-    send(unit("D", 3))
-    heard(fr.at[1], 7)
-    greet(fr.at[2])
-    send(unit("C", 0))
-    send(unit("C", 2))
-    send(unit("N", 3))
-    send(unit("N", 1))
-    heard(fr.at[2], 7)
-    greet_along_z(f1)
-
-    def interleaved(re, im, out):
-        out[pl.ds(0, ORB, 2), :] = re
-        out[pl.ds(1, ORB, 2), :] = im
+    def send(pair, t):
+        two = pl.ds(pair[0], 2)
+        q, n = quarter(t), pair[0] // 2
+        x_sends.append(
+            to_cell(ub.at[q, two], rb.at[q, two], xs.at[t, n], xr.at[t, n], pair[1], 0)
+        )
+
+    def x_arrived(pair, t):
+        two = rb.at[quarter(t), pl.ds(pair[0], 2)]
+        pltpu.make_async_copy(two, two, xr.at[t, pair[0] // 2]).wait()
+
+    def relay(t):
+        q = quarter(t)
+        for d, c_pair in ((RD, RC), (LD, LC)):
+            x_arrived(d, t)
+            two = pl.ds(c_pair[0], 2)
+            total = ub[q, two].astype(F32) + rb[q, pl.ds(d[0], 2)].astype(F32)
+            ub[q, two] = total.astype(BF16)
+            send(c_pair, t)
+
+    def along_z(t):
+        q = quarter(t)
+        for pair in (RN, LN, RC, LC):
+            x_arrived(pair, t)
+        total = own[q] + rb[q, pl.ds(2, 4)].astype(F32) + rb[q, pl.ds(8, 4)].astype(F32)
+        own[q] = total
+        zb[q] = total.astype(BF16)
+        for d in (2, 3, 1):
+            zi = lax.bitwise_xor(z, d)
+            pltpu.make_async_remote_copy(
+                src_ref=zb.at[q, zi], dst_ref=zr.at[q, z], send_sem=zs, recv_sem=zrs.at[t, d - 1],
+                device_id={"cell": x * NZ + zi}, device_id_type=MESH,
+            ).start()
 
     def send_plane(src, dst, ssem, rsem, dz):
         @pl.loop(1 if dz == 0 else 0, 8)
@@ -186,59 +188,83 @@
         part_of = buf.at[pl.ds(0, NE - 1)]
         pltpu.make_async_copy(part_of, part_of, sem).wait()
 
-    send(unit("C", 1))
-    send(unit("C", 3))
+    def to_energies(t):
+        q = quarter(t)
+        total = own[q, z]
+        for d in (1, 3, 2):
+            n = lax.bitwise_xor(z, d)
+            pltpu.make_async_copy(zr.at[q, n], zr.at[q, n], zrs.at[t, d - 1]).wait()
+            total = total + zr[q, n].astype(F32)
+        il[pl.ds(0, ROWS, 2), :] = total[0]
+        il[pl.ds(1, ROWS, 2), :] = total[1]
+        tiles = pl.ds(q * 8, 8)
+        lb[tiles, 0] = il[...].reshape(8, 8, ORB).astype(BF16)
+        lb[tiles, 1] = (il[...] + db[q]).reshape(8, 8, ORB).astype(BF16)
+        if ORDER[t] == 0:
+            lr[e] = lb[e]
+        send_plane(lb, lr, es, er, ORDER[t])
+
+    mids(2)
+    terms(RD, 2, 0)
+    terms(LD, 2, 2)
+    heard(barrier, 7)
+    greet(fr.at[0])
+    send(RD, 0)
+    send(LD, 0)
+    mids(1)
+    terms(RN, 1, 2)
+    send(RN, 0)
+    mids(3)
+    terms(LN, 3, 0)
+    send(LN, 0)
+    send(RD, 1)
+    send(LD, 1)
+    heard(fr.at[0], 7)
+    greet(fr.at[1])
+    terms(RC, 1, 0)
+    terms(LC, 3, 2)
+    relay(0)
+    send(RN, 1)
+    send(LN, 1)
+    send(RD, 2)
+    send(LD, 2)
+    heard(fr.at[1], 7)
+    greet(fr.at[2])
+    mids(0)
+    for zi in range(NZ):
+        split(part(0, zi), own, zi, F32)
+    relay(1)
+    send(RN, 2)
+    send(LN, 2)
+    send(RD, 3)
+    send(LD, 3)
+    heard(fr.at[2], 7)
+    greet_along_z(f1)
+    gr0 = gv[0, c].astype(F32)
+    gi0 = gv[1, c].astype(F32)
+    ib[pl.ds(0, ORB, 2), :] = gr0 - gr0.T
+    ib[pl.ds(1, ORB, 2), :] = gi0 + gi0.T
+    db[...] = ib[...].reshape(4, 2 * ROWS, ORB)
+    along_z(0)
+    relay(2)
+    send(RN, 3)
+    send(LN, 3)
+    along_z(1)
+    heard(f1, 2)
+    greet_along_z(f2)
+    relay(3)
 
     w_sends = []
     for n, dx in enumerate((1, 3, 2)):
         w_sends.append(to_cell(w.at[:, rows_of(dx)], wx.at[x], ws.at[n], wr.at[n], dx, 0))
 
-    mids(0)
-    for zi in range(NZ):
-        own[zi] = part(0, zi)
-    gr0 = gv[0, c].astype(F32)
-    gi0 = gv[1, c].astype(F32)
-    interleaved(gr0 - gr0.T, gi0 + gi0.T, db)
-    heard(f1, 2)
-    greet_along_z(f2)
-
-    def x_arrived(u):
-        pltpu.make_async_copy(rb.at[u], rb.at[u], xr.at[u]).wait()
-
-    for zi in (0, 2, 1, 3):
-        a = UNITS["C", zi]
-        b = UNITS["N", zi]
-        x_arrived(b)
-        x_arrived(a)
-        both = own[zi]
-        re = both[:, :ORB] + rb[a, 0].astype(F32) + rb[b, 0].astype(F32)
-        im = both[:, ORB:] + rb[a, 1].astype(F32) + rb[b, 1].astype(F32)
-        own[zi] = jnp.concatenate([re, im], axis=1)
-        zb[zi, 0] = re.astype(BF16)
-        zb[zi, 1] = im.astype(BF16)
-
-        @pl.when(zi != z)
-        def _():
-            pltpu.make_async_remote_copy(
-                src_ref=zb.at[zi], dst_ref=zr.at[z], send_sem=zs, recv_sem=zrs.at[z],
-                device_id={"cell": x * NZ + zi}, device_id_type=MESH,
-            ).start()
-
-    both = own[z]
-    re, im = both[:, :ORB], both[:, ORB:]
-    for dz in (1, 3, 2):
-        n = zof(dz)
-        pltpu.make_async_copy(zr.at[n], zr.at[n], zrs.at[n]).wait()
-        re = re + zr[n, 0].astype(F32)
-        im = im + zr[n, 1].astype(F32)
-
-    interleaved(re, im, ib)
-    lb[:, 0] = ib[...].reshape(NE, 8, ORB).astype(BF16)
-    lb[:, 1] = (ib[...] + db[...]).reshape(NE, 8, ORB).astype(BF16)
+    along_z(2)
     heard(f2, 2)
-    lr[e] = lb[e]
-    for dz in (2, 1, 3, 0):
-        send_plane(lb, lr, es, er, dz)
+    to_energies(0)
+    along_z(3)
+    to_energies(1)
+    to_energies(2)
+    to_energies(3)
 
     even = lax.rem(lax.broadcasted_iota(jnp.int32, (NE, 8, ORB), 1), 2) == 0
 
@@ -341,6 +367,16 @@
     local.wait()
 
 
+def finish(parts, pol, screened, pol_out, total, sems):
+    pol_copy = pltpu.make_async_copy(pol, pol_out, sems.at[0])
+    pol_copy.start()
+    total[...] = sum(parts[n].astype(F32) for n in range(NZ)).astype(BF16)
+    out_copy = pltpu.make_async_copy(total, screened, sems.at[1])
+    out_copy.start()
+    pol_copy.wait()
+    out_copy.wait()
+
+
 def on_device(g, s, w, coupling):
     block = (2, ORB, ORB)
     dma = pltpu.SemaphoreType.DMA
@@ -362,14 +398,15 @@
             pltpu.SMEM((NX * NZ, NX * NZ), jnp.int32),
             vm((2 * ORB, 2 * ORB), BF16),
             vm((NX, NZ, ORB, 2 * ORB), BF16),
-            vm((12, *block), BF16),
-            vm((12, *block), BF16),
-            vm((NZ, ORB, 2 * ORB), F32),
-            vm((NZ, *block), BF16),
-            vm((NZ, *block), BF16),
+            vm((4, 12, 2, ROWS, ORB), BF16),
+            vm((4, 12, 2, ROWS, ORB), BF16),
+            vm((4, NZ, 2, ROWS, ORB), F32),
+            vm((4, NZ, 2, ROWS, ORB), BF16),
+            vm((4, NZ, 2, ROWS, ORB), BF16),
             vm((2 * ORB, ORB), F32),
+            vm((2 * ROWS, ORB), F32),
             vm((NE, 2, 8, ORB), BF16),
-            vm((2 * ORB, ORB), F32),
+            vm((4, 2 * ROWS, ORB), F32),
             vm((NE, 2, 8, ORB), BF16),
             vm((NE + 8, 8, ORB), F32),
             vm((NE + 8, 8, ORB), F32),
@@ -384,10 +421,10 @@
             dma((5,)),
             dma,
             dma,
-            dma((12,)),
-            dma((12,)),
-            dma,
-            dma((NZ,)),
+            dma((4, 6)),
+            dma((4, 6)),
+            dma,
+            dma((4, 3)),
             dma,
             dma,
             dma,
@@ -406,8 +443,15 @@
         ],
         compiler_params=pltpu.CompilerParams(collective_id=0, has_side_effects=True, vmem_limit_bytes=VL),
     )(*(pltpu.with_memory_space_constraint(v, pltpu.HBM) for v in operands))
+    screened, pol = pl.pallas_call(
+        finish,
+        out_shape=(jax.ShapeDtypeStruct(block, BF16), jax.ShapeDtypeStruct((NE, 8, ORB), BF16)),
+        in_specs=[pl.BlockSpec(memory_space=pltpu.VMEM), pl.BlockSpec(memory_space=pl.ANY)],
+        out_specs=(pl.BlockSpec(memory_space=pl.ANY), pl.BlockSpec(memory_space=pl.ANY)),
+        scratch_shapes=[vm(block, BF16), dma((2,))],
+        compiler_params=pltpu.CompilerParams(vmem_limit_bytes=VL // 4),
+    )(parts, pol)
     polar = jnp.transpose(pol.reshape(ORB, 2, ORB), (1, 0, 2)).reshape(1, 2, 1, ORB * ORB)
-    screened = sum(parts[n].astype(F32) for n in range(NZ)).astype(BF16)
     return polar, screened.reshape(1, 2, 1, ORB, ORB)
 
 

time: 60.7 us -> 59.1 us (0.974)
  the two profiles are of different devices: /device:TPU:6 before, /device:TPU:1 now
where the time goes in v4:
time: 59.1 us; the launch traced here: 59 us
  Pallas kernels  58.3 us (99%)
  between operations  0.64 us (1%)
    pallas_call x1, Pallas kernels, on_device(): pl.pallas_call(kernel, out_shape=(jax.ShapeDtypeStruct((NE, 8, ORB), BF16...  57.6 us

profile of v4, /device:TPU:1, one launch (start us, length us, event | category | flops | bytes accessed | tf_op | source)
XLA Modules:
  0.0 59.0 jit_solution(12751819490994934957)
XLA Ops:
  0.6 57.6 %shard_map.59 = (bf16[32,8,128]{2,1,0:T(8,128)(2,1)S(1)}, bf16[4,2,128,128]{3,2,1,0:T(8,128)(2,1)S(1)}) custom-call(bf16[2,16,128,128]{3,2,1,0:T(8,128)(2,1)} %bitcast.11, bf16[2,128,128]{2,1,0:T(8,128)(2,1)} %bitcast.13, bf16[2,16,128,128]{3,2,1,0:T(8,128)(2,1)} %bitcast.12, s32[16,16]{1,0:T(8,128)} %cpl.1), custom_call_target="tpu_custom_call" | custom-call | tf_op jit(solution)/shard_map/pallas_call | solution.py:387
  58.3 0.7 %shard_map.60 = (bf16[2,128,128]{2,1,0:T(8,128)(2,1)}, bf16[32,8,128]{2,1,0:T(8,128)(2,1)}) custom-call(bf16[4,2,128,128]{3,2,1,0:T(8,128)(2,1)S(1)} %get-tuple-element.6.parts, bf16[32,8,128]{2,1,0:T(8,128)(2,1)S(1)} %get-tuple-element.7.pol), custom_call_target="tpu_custom_call" | custom-call | tf_op jit(solution)/shard_map/pallas_call | solution.py:446

commit v5 on v4

--- a/solution.py
+++ b/solution.py
@@ -40,7 +40,7 @@
 def kernel(
     g, s, w, cpl, pol, zout,
     gv, sv, cv, srhs, midv, ub, rb, own, zb, zr, ib, il, lb, db, lr, a1, a2, br, bi,
-    pb, pr, pg, wx, acc, z2b,
+    pb, pr, pg, prhs, wx, acc, z2b,
     ld, cld, wld, xs, xr, zs, zrs, es, er, ps, pr_, fr, f1, f2, ws, wr, gs, gr_, z2s, z2r, pols, lcl,
 ):
     e = lax.axis_index("energy")
@@ -259,9 +259,9 @@
         w_sends.append(to_cell(w.at[:, rows_of(dx)], wx.at[x], ws.at[n], wr.at[n], dx, 0))
 
     along_z(2)
+    along_z(3)
     heard(f2, 2)
     to_energies(0)
-    along_z(3)
     to_energies(1)
     to_energies(2)
     to_energies(3)
@@ -316,44 +316,46 @@
 
     z_sends = []
     recv_of = {2: 0, 3: 1, 1: 2}
-    for dx in (0, 1, 3, 2):
-        j = xof(dx)
-        if dx == 0:
-            raw = pr[...]
-        else:
-            n = recv_of[dx]
-            pltpu.make_async_copy(pg.at[j], pg.at[j], gr_.at[n]).wait()
-            raw = pg[j]
-        ib[...] = raw.astype(F32).reshape(2 * ORB, ORB)
-        rhs = stacked(ib[pl.ds(0, ORB, 2), :].astype(BF16), ib[pl.ds(1, ORB, 2), :].astype(BF16))
-        left = jnp.concatenate(
-            [wx[j, 0].reshape(NZ * ORB, ORB), wx[j, 1].reshape(NZ * ORB, ORB)], axis=1
-        )
-        mid = dot(left, rhs)
-        for zi in range(NZ):
-            weight = cv[x * NZ + zi, j * NZ + z].astype(F32)
-            midv[dx, zi] = (mid[zi * ORB : (zi + 1) * ORB] * weight).astype(BF16)
-        for n, dz in enumerate((2, 3, 1, 0)):
-            zi = lax.bitwise_xor(z, dz)
-            term = dot_t(midv[dx, zi], stacked(wx[j, 0, zi], wx[j, 1, zi]))
-            if dx == 0:
-                acc[dz] = term
-            elif dx != 2:
-                acc[dz] += term
-            else:
-                term = term + acc[dz]
-                z2b[dz, 0] = term[:, :ORB].astype(BF16)
-                z2b[dz, 1] = term[:, ORB:].astype(BF16)
-                if dz == 0:
-                    local = pltpu.make_async_copy(z2b.at[0], zout.at[z], lcl)
-                    local.start()
+    for pair in ((2, 3), (1, 0)):
+        for dx in (0, 1, 3, 2):
+            j = xof(dx)
+            if pair[0] == 2:
+                if dx == 0:
+                    raw = pr[...]
                 else:
-                    copy = pltpu.make_async_remote_copy(
-                        src_ref=z2b.at[dz], dst_ref=zout.at[z], send_sem=z2s.at[n], recv_sem=z2r.at[n],
-                        device_id={"cell": x * NZ + zi}, device_id_type=MESH,
-                    )
-                    copy.start()
-                    z_sends.append(copy)
+                    pltpu.make_async_copy(pg.at[j], pg.at[j], gr_.at[recv_of[dx]]).wait()
+                    raw = pg[j]
+                ib[...] = raw.astype(F32).reshape(2 * ORB, ORB)
+                prhs[dx] = stacked(
+                    ib[pl.ds(0, ORB, 2), :].astype(BF16), ib[pl.ds(1, ORB, 2), :].astype(BF16)
+                )
+            blocks = [lax.bitwise_xor(z, d) for d in pair]
+            left = jnp.concatenate(
+                [jnp.concatenate([wx[j, 0, zi], wx[j, 1, zi]], axis=1) for zi in blocks], axis=0
+            )
+            mid = dot(left, prhs[dx])
+            for n, (d, zi) in enumerate(zip(pair, blocks)):
+                weight = cv[x * NZ + zi, j * NZ + z].astype(F32)
+                half = (mid[n * ORB : (n + 1) * ORB] * weight).astype(BF16)
+                term = dot_t(half, stacked(wx[j, 0, zi], wx[j, 1, zi]))
+                if dx == 0:
+                    acc[d] = term
+                elif dx != 2:
+                    acc[d] += term
+                else:
+                    term = term + acc[d]
+                    z2b[d, 0] = term[:, :ORB].astype(BF16)
+                    z2b[d, 1] = term[:, ORB:].astype(BF16)
+                    if d == 0:
+                        local = pltpu.make_async_copy(z2b.at[0], zout.at[z], lcl)
+                        local.start()
+                    else:
+                        copy = pltpu.make_async_remote_copy(
+                            src_ref=z2b.at[d], dst_ref=zout.at[z], send_sem=z2s.at[d - 1],
+                            recv_sem=z2r.at[d - 1], device_id={"cell": x * NZ + zi}, device_id_type=MESH,
+                        )
+                        copy.start()
+                        z_sends.append(copy)
 
     for copy in x_sends + w_sends + g_sends + z_sends:
         copy.wait_send()
@@ -415,6 +417,7 @@
             vm((NE, 8, ORB), BF16),
             vm((NE, 8, ORB), BF16),
             vm((NX, NE, 8, ORB), BF16),
+            vm((NX, 2 * ORB, 2 * ORB), BF16),
             vm((NX, 2, NZ, ORB, ORB), BF16),
             vm((NZ, ORB, 2 * ORB), F32),
             vm((NZ, *block), BF16),

time: 59.1 us -> 58.2 us (0.985)
  Pallas kernels: 58.3 us -> 57.4 us
    pallas_call x1, Pallas kernels: 57.6 us -> 56.8 us  [on_device(): pl.pallas_call(kernel, out_shape=(jax.ShapeDtypeStruct((NE, 8, ORB), BF16...]
where the time goes in v5:
time: 58.2 us; the launch traced here: 58.1 us
  Pallas kernels  57.4 us (99%)
  between operations  0.64 us (1%)
    pallas_call x1, Pallas kernels, on_device(): pl.pallas_call(kernel, out_shape=(jax.ShapeDtypeStruct((NE, 8, ORB), BF16...  56.8 us

profile of v5, /device:TPU:1, one launch (start us, length us, event | category | flops | bytes accessed | tf_op | source)
XLA Modules:
  0.0 58.1 jit_solution(2585904836770371294)
XLA Ops:
  0.6 56.8 %shard_map.59 = (bf16[32,8,128]{2,1,0:T(8,128)(2,1)S(1)}, bf16[4,2,128,128]{3,2,1,0:T(8,128)(2,1)S(1)}) custom-call(bf16[2,16,128,128]{3,2,1,0:T(8,128)(2,1)} %bitcast.11, bf16[2,128,128]{2,1,0:T(8,128)(2,1)} %bitcast.13, bf16[2,16,128,128]{3,2,1,0:T(8,128)(2,1)} %bitcast.12, s32[16,16]{1,0:T(8,128)} %cpl.1), custom_call_target="tpu_custom_call" | custom-call | tf_op jit(solution)/shard_map/pallas_call | solution.py:389
  57.4 0.7 %shard_map.60 = (bf16[2,128,128]{2,1,0:T(8,128)(2,1)}, bf16[32,8,128]{2,1,0:T(8,128)(2,1)}) custom-call(bf16[4,2,128,128]{3,2,1,0:T(8,128)(2,1)S(1)} %get-tuple-element.6.parts, bf16[32,8,128]{2,1,0:T(8,128)(2,1)S(1)} %get-tuple-element.7.pol), custom_call_target="tpu_custom_call" | custom-call | tf_op jit(solution)/shard_map/pallas_call | solution.py:449
